TPU v7x, 128 devices: a whole 4x4x4 slice. The times are simulated.
128 devices in a mesh: param: 4 (over z_lo, core), space: 32 (over y, z_hi, x).
Axes of the slice: x: 4, y: 4, z: 4 (z_hi: 2, z_lo: 2; z = z_hi * 2 + z_lo), core: 2. Of those that a mesh axis runs over, the one named last changes fastest.
Arguments:
- fine_state: bfloat16 [64, 16, 64, 512], P('space', None, None, 'param'), may hold values from -6 to 6
- fine_tangent: bfloat16 [64, 16, 64, 512], P('space', None, None, 'param'), may hold values from -6 to 6
- down_weight: float32 [8, 512, 1024], P(None, 'space', 'param'), may hold values from -0.09375 to 0.09375
- conv_weight: float32 [27, 1024, 1024], P(None, 'space', 'param'), may hold values from -0.0390625 to 0.0390625
- up_weight: float32 [8, 1024, 512], P(None, 'space', 'param'), may hold values from -0.1875 to 0.1875
Outputs:
- state_out: bfloat16 [64, 16, 64, 512], P('space', None, None, 'param')
- tangent_out: bfloat16 [64, 16, 64, 512], P('space', None, None, 'param')
All inputs are finite; a program needn't handle non-finite values.
Results may differ from a plain program's by a relative error of at most 0.0075.
Values may be sent and summed in bfloat16 or wider, within the bound.
A program may use at most 128 MiB of HBM per device.

v0:
```python
import jax
import jax.numpy as jnp
from jax import lax
from jax.sharding import PartitionSpec as P


def padded_2(block, sides, width):
    for axis, dim in sides:
        count = lax.axis_size(axis)
        forward = [(i, i + 1) for i in range(count - 1)]
        backward = [(target, source) for source, target in forward]
        low = lax.ppermute(
            lax.slice_in_dim(block, block.shape[dim] - width, None, axis=dim), axis, forward
        )
        high = lax.ppermute(lax.slice_in_dim(block, 0, width, axis=dim), axis, backward)
        block = jnp.concatenate([low, block, high], axis=dim)
    return block


def silu_pair(primal, tangent):
    sigma = jax.nn.sigmoid(primal)
    return (primal * sigma, sigma * (1.0 + primal * (1.0 - sigma)) * tangent)


def cube_block(source, kernel, planes):
    span_y = source.shape[2] - 2
    span_x = source.shape[3] - 2
    width = source.shape[4]
    result = None
    for tap_z in range(3):
        for tap_y in range(3):
            window = jnp.stack(
                [
                    source[
                        :, tap_z : tap_z + planes, tap_y : tap_y + span_y, tap_x : tap_x + span_x, :
                    ]
                    for tap_x in range(3)
                ],
                axis=4,
            )
            window = window.reshape(-1, 3 * width)
            first_tap = 9 * tap_z + 3 * tap_y
            weights = kernel[first_tap : first_tap + 3].reshape(3 * width, kernel.shape[2])
            term = jnp.dot(window, weights, preferred_element_type=jnp.float32)
            result = term if result is None else result + term
    return result


def local(fine_state, fine_tangent, down_weight, conv_weight, up_weight):
    planes = fine_state.shape[0] // 2
    span_y = fine_state.shape[1] // 2
    span_x = fine_state.shape[2] // 2
    cells = planes * span_y * span_x
    state_full, tangent_full = (
        lax.all_gather(fine_state, "param", axis=3, tiled=True),
        lax.all_gather(fine_tangent, "param", axis=3, tiled=True),
    )
    wide_fine = state_full.shape[3]
    paired = jnp.stack([state_full, tangent_full], axis=0)
    patches = (
        paired.reshape(2, planes, 2, span_y, 2, span_x, 2, wide_fine)
        .transpose(0, 1, 3, 5, 2, 4, 6, 7)
        .reshape(2 * cells, 8, wide_fine)
    )
    down_kernel = down_weight.astype(jnp.bfloat16)
    up_kernel = up_weight.astype(jnp.bfloat16)
    cube_kernel = conv_weight.astype(jnp.bfloat16)
    coarse_local = down_weight.shape[2]
    fine_local = up_weight.shape[2]
    portion = lax.all_gather(down_kernel, "space", axis=1, tiled=True)
    width = portion.shape[1]
    columns = patches.reshape(2 * cells, 8 * width)
    first_pre = jnp.dot(
        columns, portion.reshape(8 * width, portion.shape[2]), preferred_element_type=jnp.float32
    )
    first_pre = first_pre.reshape(2, cells, coarse_local)
    first_val, first_dir = silu_pair(first_pre[0], first_pre[1])
    first_round = jnp.stack(
        [first_val.astype(jnp.bfloat16), first_dir.astype(jnp.bfloat16)], axis=0
    )
    first_stack = first_round.reshape(2, planes, span_y, span_x, coarse_local)
    haloed = padded_2(first_stack, (("space", 1),), 1)
    every_channel = lax.all_gather(haloed, "param", axis=4, tiled=True)
    padded = jnp.pad(every_channel, ((0, 0), (0, 0), (1, 1), (1, 1), (0, 0)))
    second_pre = cube_block(
        padded, lax.all_gather(cube_kernel, "space", axis=1, tiled=True), planes
    ).reshape(2, cells, coarse_local)
    second_val, second_dir = silu_pair(second_pre[0], second_pre[1])
    second_val = second_val + first_round[0].astype(jnp.float32)
    second_dir = second_dir + first_round[1].astype(jnp.float32)
    top_stack = jnp.stack(
        [second_val.astype(jnp.bfloat16), second_dir.astype(jnp.bfloat16)], axis=0
    )
    top_full = lax.all_gather(top_stack, "param", axis=2, tiled=True)
    top_rows = top_full.reshape(2 * cells, top_full.shape[2])
    portion = lax.all_gather(up_kernel, "space", axis=1, tiled=True)
    width = portion.shape[1]
    columns = top_rows
    product = jnp.dot(
        columns,
        portion.transpose(1, 0, 2).reshape(width, 8 * fine_local),
        preferred_element_type=jnp.float32,
    )
    shaped = product.reshape(2, planes, span_y, span_x, 2, 2, 2, fine_local).transpose(
        0, 1, 4, 2, 5, 3, 6, 7
    )
    outputs = shaped.reshape(2, 2 * planes, 2 * span_y, 2 * span_x, fine_local).astype(jnp.bfloat16)
    return (outputs[0], outputs[1])


def solution(mesh):
    in_specs = (
        P("space", None, None, "param"),
        P("space", None, None, "param"),
        P(None, "space", "param"),
        P(None, "space", "param"),
        P(None, "space", "param"),
    )
    out_specs = (P("space", None, None, "param"), P("space", None, None, "param"))
    return jax.shard_map(local, mesh=mesh, in_specs=in_specs, out_specs=out_specs, check_vma=False)
```

profile of v0, /device:TPU:1, one launch (start us, length us, event | category | flops | bytes accessed | tf_op | source)
XLA Modules:
  0.0 463.8 jit_solution(5521071083884901412)
XLA Ops:
  8.7 1.5 convert_element_type.39
  10.3 32.1 %all-gather.8.cloned.1.call-done = bf16[2,16,64,512]{3,2,1,0:T(8,128)(2,1)} async-done(((bf16[2,16,64,128]{3,2,1,0:T(8,128)(2,1)}), bf16[2,16,64,512]{3,2,1,0:T(8,128)(2,1)}) %all-gather.8.cloned.1.call-update) | async-done | bytes 2097168 | tf_op jit(solution)/shard_map/all_gather | solution.py:55
  42.4 2.7 stack.135
  45.1 28.9 %all-gather.10.cloned.1.call-done = bf16[2,16,64,512]{3,2,1,0:T(8,128)(2,1)} async-done(((bf16[2,16,64,128]{3,2,1,0:T(8,128)(2,1)}), bf16[2,16,64,512]{3,2,1,0:T(8,128)(2,1)}) %all-gather.10.cloned.1.call-update) | async-done | bytes 2097168 | tf_op jit(solution)/shard_map/all_gather | solution.py:56
  74.0 4.1 stack.136
  78.1 7.8 %copy_bitcast_fusion = bf16[2,1,8,32,2,2,2,512]{7,6,5,4,3,2,0,1:T(2,128)(2,1)} fusion(bf16[1,1,2,8,2,32,2,512]{7,6,5,4,3,2,1,0:T(2,128)(2,1)} %stack.136, bf16[1,1,2,8,2,32,2,512]{7,6,5,4,3,2,1,0:T(2,128)(2,1)S(1)} %stack.135), kind=kLoop, calls=%fused_computation.25 | loop fusion | flops 2097152 | bytes 8388608 | tf_op jit(solution)/shard_map/transpose | solution.py:62
  85.9 7.9 %reshape_reshape.3 = bf16[512,4096]{1,0:T(8,128)(2,1)} reshape(bf16[2,1,8,32,2,2,2,512]{7,6,5,4,3,2,0,1:T(2,128)(2,1)} %copy_bitcast_fusion) | data formatting | bytes 8388608 | tf_op jit(solution)/shard_map/reshape;reshape | solution.py:72
  93.8 56.8 %all-gather.12.cloned.1.call-done = bf16[8,512,256]{2,1,0:T(8,128)(2,1)} async-done(((bf16[8,16,256]{2,1,0:T(8,128)(2,1)}), bf16[8,512,256]{2,1,0:T(8,128)(2,1)}) %all-gather.12.cloned.1.call-update) | async-done | bytes 2097168 | tf_op jit(solution)/shard_map/all_gather | solution.py:70
  150.6 4.1 fusion.32
  154.9 1.4 collective-permute-start.1
  156.3 4.0 collective-permute-start
  160.3 2.5 collective-permute-done.1
  166.4 42.7 %all-gather.14.cloned.1.call-done = bf16[2,3,8,32,1024]{4,3,2,0,1:T(8,128)(2,1)} async-done(((bf16[2,3,8,32,256]{4,3,2,0,1:T(8,128)(2,1)}), bf16[2,3,8,32,1024]{4,3,2,0,1:T(8,128)(2,1)}) %all-gather.14.cloned.1.call-update) | async-done | bytes 3145744 | tf_op jit(solution)/shard_map/all_gather | solution.py:83
  209.1 5.3 %fusion.23 = (bf16[2,1,8,32,1,1024]{5,3,2,0,4,1:T(8,128)(2,1)S(1)}, bf16[2,1,8,32,1,1024]{5,3,2,0,4,1:T(8,128)(2,1)S(1)}, bf16[2,1,8,32,1,1024]{5,3,2,0,4,1:T(8,...) fusion(bf16[2,3,8,32,1024]{4,3,2,0,1:T(8,128)(2,1)} %all-gather, ...), kind=kLoop, calls=%fused_computation.67 | loop fusion | bytes 14680064 | tf_op jit(solution)/shard_map/stack | solution.py:32
  214.8 2.7 copy.54
  217.5 3.4 copy.70
  220.9 7.1 %fusion.22 = (bf16[2,1,8,32,1,1024]{5,3,2,0,4,1:T(8,128)(2,1)}, bf16[2,1,8,32,1,1024]{5,3,2,0,4,1:T(8,128)(2,1)}, bf16[2,1,8,32,1,1024]{5,3,2,0,4,1:T(8,128)(2,1...) fusion(bf16[2,3,8,32,1024]{4,3,2,0,1:T(8,128)(2,1)S(1)} %copy-done), kind=kLoop, calls=%fused_computation.66 | loop fusion | bytes 23068672 | tf_op jit(solution)/shard_map/stack | solution.py:32
  228.1 2.8 pad_maximum_fusion.7
  230.8 2.7 copy.53
  233.6 3.4 copy.69
  237.0 2.7 copy.55
  239.8 3.4 copy.71
  243.2 1.1 pad_maximum_fusion.1
  244.4 2.7 copy.47
  247.1 3.5 copy.63
  250.6 2.7 copy.48
  253.4 3.6 copy.64
  257.9 2.7 copy.51
  260.7 3.4 copy.67
  264.0 2.7 copy.52
  266.8 3.4 copy.68
  271.2 2.7 copy.49
  274.0 3.4 copy.65
  277.4 2.7 copy.50
  280.1 3.4 copy.66
  283.5 73.8 %all-gather.16.cloned.1.call-done = bf16[27,1024,256]{2,1,0:T(8,128)(2,1)} async-done(((bf16[27,32,256]{2,1,0:T(8,128)(2,1)}), bf16[27,1024,256]{2,1,0:T(8,128)(2,1)}) %all-gather.16.cloned.1.call-update) | async-done | bytes 14155792 | tf_op jit(solution)/shard_map/all_gather | solution.py:86
  357.3 6.2 %fusion.30 = (bf16[3,1024,256]{2,1,0:T(8,128)(2,1)S(1)}, bf16[3,1024,256]{2,1,0:T(8,128)(2,1)S(1)}, bf16[3,1024,256]{2,1,0:T(8,128)(2,1)S(1)}, bf16[3,1024,256]{...) fusion(bf16[27,1024,256]{2,1,0:T(8,128)(2,1)} %all-gather.16.cl, ...), kind=kLoop, calls=%fused_computation.87 | loop fusion | bytes 28311552 | tf_op jit(solution)/shard_map/slice | solution.py:43
  366.7 1.0 convolution_add_fusion.6
  368.4 1.0 convolution_add_fusion.5
  371.4 1.0 convolution_add_fusion.3
  374.4 1.0 convolution_add_fusion.1
  375.9 1.0 convolution_add_fusion
  377.8 52.1 %all-gather.20.cloned.1.call-done = bf16[8,1024,128]{2,0,1:T(8,128)(2,1)} async-done(((bf16[8,32,128]{2,0,1:T(8,128)(2,1)}), bf16[8,1024,128]{2,0,1:T(8,128)(2,1)}) %all-gather.20.cloned.1.call-update) | async-done | bytes 2097168 | tf_op jit(solution)/shard_map/all_gather | solution.py:96
  429.9 3.2 copy.57
  433.1 18.1 %all-gather.18.cloned.1.call-done = bf16[2,256,1024]{2,1,0:T(8,128)(2,1)} async-done(((bf16[2,256,256]{2,1,0:T(8,128)(2,1)}), bf16[2,256,1024]{2,1,0:T(8,128)(2,1)}) %all-gather.18.cloned.1.call-update) | async-done | bytes 1048592 | tf_op jit(solution)/shard_map/all_gather | solution.py:94
  451.2 2.5 fusion
  453.8 1.3 copy.59
  455.2 1.3 copy.58
  (80 shorter events, 16.7 us)
Async XLA Ops:
  7.2 35.2 %all-gather.8.cloned.1.call-start = ((), (), s32[]{:S(2)}) async-start(), calls=%async_computation | async-start | bytes 2621440 | tf_op jit(solution)/shard_map/all_gather | solution.py:55
  7.9 66.1 %all-gather.10.cloned.1.call-start = ((), (), s32[]{:S(2)}) async-start(), calls=%async_computation.1 | async-start | bytes 2621440 | tf_op jit(solution)/shard_map/all_gather | solution.py:56
  8.6 141.9 %all-gather.12.cloned.1.call-start = ((), (), s32[]{:S(2)}) async-start(), calls=%async_computation.2 | async-start | bytes 2162688 | tf_op jit(solution)/shard_map/all_gather | solution.py:70
  10.3 198.8 %all-gather.14.cloned.1.call-start = ((), (), s32[]{:S(2)}) async-start(), calls=%async_computation.3 | async-start | bytes 3932160 | tf_op jit(solution)/shard_map/all_gather | solution.py:83
  154.7 10.0 %copy-start.23 = (f32[27,32,256]{2,1,0:T(8,128)S(1)}, f32[27,32,256]{2,1,0:T(8,128)}, u32[]{:S(2)}) copy-start(f32[27,32,256]{2,1,0:T(8,128)} %param.8) | copy-start | bytes 2654212
  154.7 10.9 %copy-start.24 = (f32[8,32,128]{2,1,0:T(8,128)S(1)}, f32[8,32,128]{2,1,0:T(8,128)}, u32[]{:S(2)}) copy-start(f32[8,32,128]{2,1,0:T(8,128)} %param.9) | copy-start | bytes 393220
  154.9 7.9 %collective-permute-start.1 = (bf16[2,1,8,32,256]{4,3,2,0,1:T(8,128)(2,1)S(1)}, bf16[2,1,8,32,256]{4,3,2,0,1:T(8,128)(2,1)S(1)}, u32[]{:S(2)}, u32[]{:S(2)}) collective-permute-start(bf16[2,1,8,32,256]{4,3,2,0,1:T(8,128)(2,1)S(1)} %pad_maximum_fusion.11), channel_id=1, source_target_pairs={{1,0},{2,1},{3,2},{4,3},{5,4},{6,5},{7,6},{8,7},{9,8},{10,9},{11,1... | collective-permute-start | bytes 786440 | tf_op jit(solution)/shard_map/ppermute | solution.py:15
  156.3 7.3 %collective-permute-start = (bf16[2,1,8,32,256]{4,3,2,0,1:T(8,128)(2,1)S(1)}, bf16[2,1,8,32,256]{4,3,2,0,1:T(8,128)(2,1)S(1)}, u32[]{:S(2)}, u32[]{:S(2)}) collective-permute-start(bf16[2,1,8,32,256]{4,3,2,0,1:T(8,128)(2,1)S(1)} %pad_maximum_fusion.11), channel_id=1, source_target_pairs={{0,1},{1,2},{2,3},{3,4},{4,5},{5,6},{6,7},{7,8},{8,9},{9,10},{10,1... | collective-permute-start | bytes 786440 | tf_op jit(solution)/shard_map/ppermute | solution.py:12
  164.6 192.7 %all-gather.16.cloned.1.call-start = ((), (), s32[]{:S(2)}) async-start(), calls=%async_computation.4 | async-start | bytes 14598144 | tf_op jit(solution)/shard_map/all_gather | solution.py:86
  165.5 264.3 %all-gather.20.cloned.1.call-start = ((), (), s32[]{:S(2)}) async-start(), calls=%async_computation.6 | async-start | bytes 2162688 | tf_op jit(solution)/shard_map/all_gather | solution.py:96
  166.3 284.9 %all-gather.18.cloned.1.call-start = ((), (), s32[]{:S(2)}) async-start(), calls=%async_computation.5 | async-start | bytes 1310720 | tf_op jit(solution)/shard_map/all_gather | solution.py:94
  217.5 3.4 copy-start
  239.7 3.5 copy-start.10
  239.7 3.5 copy-start.11
  239.8 3.5 copy-start.12
  239.8 3.4 copy-start.13
  253.3 3.6 copy-start.5
  253.3 3.6 copy-start.6
  253.4 3.6 copy-start.7
  253.4 3.6 copy-start.8
  253.4 3.6 copy-start.9
  266.8 3.5 copy-start.1
  266.8 3.5 copy-start.2
  266.8 3.5 copy-start.3
  266.8 3.5 copy-start.4
  283.5 80.1 %copy-start.17 = (bf16[64,8,3,1024]{3,1,2,0:T(8,128)(2,1)S(1)}, bf16[64,8,3,1024]{3,1,2,0:T(8,128)(2,1)}, u32[]{:S(2)}) copy-start(bf16[64,8,3,1024]{3,1,2,0:T(8,128)(2,1)} %copy.63) | copy-start | bytes 9437188
  363.5 1.9 copy-start.18
  364.6 2.1 copy-start.21
  366.4 1.9 copy-start.22
  367.7 2.1 copy-start.19
  369.4 2.0 copy-start.20
  370.8 2.0 copy-start.16
  372.4 2.0 copy-start.14
  373.8 2.0 copy-start.15
Sparse Core Ops, SparseCore 0:
  9.7 32.6 all-gather.7
  44.0 29.9 all-gather.9
  77.4 73.1 all-gather.11
  164.7 44.3 all-gather.13
  212.5 144.7 all-gather.15
  360.8 69.0 all-gather.19
  432.1 19.0 all-gather.17
where the time goes:
time: 473 us; the launch traced here: 464 us
  waiting for transfers between devices  309 us (65%)
  local copies, waits for them, and re-layouts  99.9 us (21%)
  other arithmetic  18.2 us (4%)
  matrix products  15.6 us (3%)
  between operations  15.1 us (3%)
  starting transfers between devices  5.71 us (1%)
    all_gather x1, waiting for transfers between devices, local(): lax.all_gather(cube_kernel, 'space', axis=1, tiled=True)  73.8 us
    all_gather x1, waiting for transfers between devices, local(): portion = lax.all_gather(down_kernel, 'space', axis=1, tiled=True)  56.8 us
    all_gather x1, waiting for transfers between devices, local(): portion = lax.all_gather(up_kernel, 'space', axis=1, tiled=True)  52.1 us
    all_gather x1, waiting for transfers between devices, local(): every_channel = lax.all_gather(haloed, 'param', axis=4, tiled=True)  42.7 us
    another operation x11, local copies, waits for them, and re-layouts, cube_block(): jnp.stack([source[:, tap_z:tap_z + planes, tap_y:tap_y + span_y, tap_x:ta...  37 us
    unnamed x60, local copies, waits for them, and re-layouts  35.9 us
    all_gather x1, waiting for transfers between devices, local(): lax.all_gather(fine_state, 'param', axis=3, tiled=True)  32.1 us
    all_gather x1, waiting for transfers between devices, local(): lax.all_gather(fine_tangent, 'param', axis=3, tiled=True)  28.9 us
  transfers between devices with their start and end apart: 9, of which 9 were waited for; matrix products, arithmetic and copies ran while one was open for 26% of the time, Pallas kernels for 0%

commit v1 on v0

--- a/solution.py
+++ b/solution.py
@@ -52,7 +52,9 @@
     span_x = fine_state.shape[2] // 2
     cells = planes * span_y * span_x
     state_full, tangent_full = (
-        lax.all_gather(fine_state, "param", axis=3, tiled=True),
+        jnp.concatenate(
+            lax.all_to_all(jnp.stack([fine_state] * lax.axis_size("param")), "param", 0, 0), axis=3
+        ),
         lax.all_gather(fine_tangent, "param", axis=3, tiled=True),
     )
     wide_fine = state_full.shape[3]

time: 473 us -> 452 us (0.956); the launches traced: 464 us -> 448 us
  waiting for transfers between devices: 309 us -> 241 us
  blocking collectives: 0 us -> 43.9 us
  local copies, waits for them, and re-layouts: 99.9 us -> 109 us
    all_to_all x0 -> x1, blocking collectives: none -> 43.9 us  [local(): lax.all_to_all(jnp.stack([fine_state] * lax.axis_size('param')), 'param',...]
    all_gather x1 -> x0, waiting for transfers between devices: 32.1 us -> none  [local(): lax.all_gather(fine_state, 'param', axis=3, tiled=True)]
    all_gather x1, waiting for transfers between devices: 28.9 us -> 0.01 us  [local(): lax.all_gather(fine_tangent, 'param', axis=3, tiled=True)]
    all_gather x1, waiting for transfers between devices: 56.8 us -> 50.5 us  [local(): portion = lax.all_gather(down_kernel, 'space', axis=1, tiled=True)]
    transpose x0 -> x1, local copies, waits for them, and re-layouts: none -> 5.37 us  [local(): patches = paired.reshape(2, planes, 2, span_y, 2, span_x, 2, wide_fine).t...]
    unnamed x60 -> x62, local copies, waits for them, and re-layouts: 35.9 us -> 35.9 us
  transfers between devices with their start and end apart: 9 -> 8, of which waited for: 9 -> 7; matrix products, arithmetic and copies ran while one was open for 26% -> 29% of each run, Pallas kernels for 0% -> 0%
where the time goes in v1:
time: 452 us; the launch traced here: 448 us
  waiting for transfers between devices  241 us (53%)
  local copies, waits for them, and re-layouts  109 us (24%)
  blocking collectives  43.9 us (10%)
  other arithmetic  18.3 us (4%)
  matrix products  15.6 us (3%)
  between operations  14.9 us (3%)
  starting transfers between devices  5.67 us (1%)
    all_gather x1, waiting for transfers between devices, local(): lax.all_gather(cube_kernel, 'space', axis=1, tiled=True)  73.4 us
    all_gather x1, waiting for transfers between devices, local(): portion = lax.all_gather(up_kernel, 'space', axis=1, tiled=True)  52.1 us
    all_gather x1, waiting for transfers between devices, local(): portion = lax.all_gather(down_kernel, 'space', axis=1, tiled=True)  50.5 us
    all_to_all x1, blocking collectives, local(): lax.all_to_all(jnp.stack([fine_state] * lax.axis_size('param')), 'param',...  43.9 us
    all_gather x1, waiting for transfers between devices, local(): every_channel = lax.all_gather(haloed, 'param', axis=4, tiled=True)  42.7 us
    another operation x11, local copies, waits for them, and re-layouts, cube_block(): jnp.stack([source[:, tap_z:tap_z + planes, tap_y:tap_y + span_y, tap_x:ta...  37.5 us
    unnamed x62, local copies, waits for them, and re-layouts  35.9 us
    all_gather x1, waiting for transfers between devices, local(): top_full = lax.all_gather(top_stack, 'param', axis=2, tiled=True)  17.9 us
  transfers between devices with their start and end apart: 8, of which 7 were waited for; matrix products, arithmetic and copies ran while one was open for 29% of the time, Pallas kernels for 0%

profile of v1, /device:TPU:1, one launch (start us, length us, event | category | flops | bytes accessed | tf_op | source)
XLA Modules:
  0.0 448.1 jit_solution(6583834059659654540)
XLA Ops:
  7.9 1.5 convert_element_type.39
  9.6 1.6 stack.141
  11.1 43.9 %all_to_all.5 = bf16[4,2,16,64,128]{4,3,2,1,0:T(8,128)(2,1)S(1)} all-to-all(bf16[4,2,16,64,128]{4,3,2,1,0:T(8,128)(2,1)S(1)} %stack.141), channel_id=1, replica_groups=mesh['param'=4,'space'=32] {'param'}, dimensions={0} | all-to-all | bytes 4194304 | tf_op jit(solution)/shard_map/all_to_all | solution.py:56
  55.0 2.0 copy.41
  57.0 2.2 stack.142
  59.2 4.5 %stack.143 = bf16[1,1,2,8,2,32,2,512]{7,6,5,4,3,2,1,0:T(2,128)(2,1)} reshape(bf16[2,16,64,512]{3,2,1,0:T(8,128)(2,1)} %all-gather.7.cloned.1.call-done) | data formatting | bytes 4194304 | tf_op jit(solution)/shard_map/stack | solution.py:61
  63.8 7.9 %maximum_bitcast_fusion = bf16[2,1,8,32,2,2,2,512]{7,6,3,5,2,4,1,0:T(2,128)(2,1)S(1)} fusion(bf16[1,1,2,8,2,32,2,512]{7,6,5,4,3,2,1,0:T(2,128)(2,1)} %stack.143, bf16[1,1,2,8,2,32,2,512]{7,6,5,4,3,2,1,0:T(2,128)(2,1)S(1)} %copy-done.1), kind=kLoop, calls=%fused_computation.24 | loop fusion | flops 2097152 | bytes 8388608 | tf_op jit(solution)/shard_map/transpose | solution.py:64
  71.6 5.4 %copy.42 = bf16[2,1,8,32,2,2,2,512]{7,6,5,4,3,2,0,1:T(2,128)(2,1)} copy(bf16[2,1,8,32,2,2,2,512]{7,6,3,5,2,4,1,0:T(2,128)(2,1)S(1)} %maximum_bitcast_fusion) | data formatting | bytes 8388608 | tf_op jit(solution)/shard_map/transpose | solution.py:64
  77.0 7.8 %reshape_reshape.3 = bf16[512,4096]{1,0:T(8,128)(2,1)} reshape(bf16[2,1,8,32,2,2,2,512]{7,6,5,4,3,2,0,1:T(2,128)(2,1)} %copy.42) | data formatting | bytes 8388608 | tf_op jit(solution)/shard_map/reshape;reshape | solution.py:74
  84.8 50.5 %all-gather.9.cloned.1.call-done = bf16[8,512,256]{2,1,0:T(8,128)(2,1)} async-done(((bf16[8,16,256]{2,1,0:T(8,128)(2,1)}), bf16[8,512,256]{2,1,0:T(8,128)(2,1)}) %all-gather.9.cloned.1.call-update) | async-done | bytes 2097168 | tf_op jit(solution)/shard_map/all_gather | solution.py:72
  135.2 4.1 fusion.32
  139.5 1.4 collective-permute-start.1
  141.0 4.0 collective-permute-start
  145.0 2.5 collective-permute-done.1
  151.0 42.7 %all-gather.11.cloned.1.call-done = bf16[2,3,8,32,1024]{4,3,2,0,1:T(8,128)(2,1)} async-done(((bf16[2,3,8,32,256]{4,3,2,0,1:T(8,128)(2,1)}), bf16[2,3,8,32,1024]{4,3,2,0,1:T(8,128)(2,1)}) %all-gather.11.cloned.1.call-update) | async-done | bytes 3145744 | tf_op jit(solution)/shard_map/all_gather | solution.py:85
  193.8 5.8 %fusion.23 = (bf16[2,1,8,32,1,1024]{5,3,2,0,4,1:T(8,128)(2,1)S(1)}, bf16[2,1,8,32,1,1024]{5,3,2,0,4,1:T(8,128)(2,1)S(1)}, bf16[2,1,8,32,1,1024]{5,3,2,0,4,1:T(8,...) fusion(bf16[2,3,8,32,1024]{4,3,2,0,1:T(8,128)(2,1)} %all-gather, ...), kind=kLoop, calls=%fused_computation.66 | loop fusion | bytes 14680064 | tf_op jit(solution)/shard_map/stack | solution.py:32
  199.9 2.7 copy.52
  202.7 3.4 copy.67
  206.1 7.1 %fusion.22 = (bf16[2,1,8,32,1,1024]{5,3,2,0,4,1:T(8,128)(2,1)}, bf16[2,1,8,32,1,1024]{5,3,2,0,4,1:T(8,128)(2,1)}, bf16[2,1,8,32,1,1024]{5,3,2,0,4,1:T(8,128)(2,1...) fusion(bf16[2,3,8,32,1024]{4,3,2,0,1:T(8,128)(2,1)S(1)} %copy-done), kind=kLoop, calls=%fused_computation.65 | loop fusion | bytes 23068672 | tf_op jit(solution)/shard_map/stack | solution.py:32
  213.2 2.7 pad_maximum_fusion.6
  215.9 2.7 copy.51
  218.6 3.4 copy.66
  222.1 2.7 copy.53
  224.8 3.4 copy.68
  229.2 2.7 copy.45
  232.0 3.5 copy.60
  235.5 2.7 copy.46
  238.2 3.6 copy.61
  241.9 1.1 pad_maximum_fusion.4
  243.0 2.7 copy.49
  245.7 3.4 copy.64
  249.1 2.7 copy.50
  251.9 3.4 copy.65
  256.3 2.7 copy.47
  259.0 3.4 copy.62
  262.4 2.7 copy.48
  265.2 3.4 copy.63
  268.5 73.4 %all-gather.13.cloned.1.call-done = bf16[27,1024,256]{2,1,0:T(8,128)(2,1)} async-done(((bf16[27,32,256]{2,1,0:T(8,128)(2,1)}), bf16[27,1024,256]{2,1,0:T(8,128)(2,1)}) %all-gather.13.cloned.1.call-update) | async-done | bytes 14155792 | tf_op jit(solution)/shard_map/all_gather | solution.py:88
  342.0 6.2 %fusion.30 = (bf16[3,1024,256]{2,1,0:T(8,128)(2,1)S(1)}, bf16[3,1024,256]{2,1,0:T(8,128)(2,1)S(1)}, bf16[3,1024,256]{2,1,0:T(8,128)(2,1)S(1)}, bf16[3,1024,256]{...) fusion(bf16[27,1024,256]{2,1,0:T(8,128)(2,1)} %all-gather.13.cl, ...), kind=kLoop, calls=%fused_computation.86 | loop fusion | bytes 28311552 | tf_op jit(solution)/shard_map/slice | solution.py:43
  353.0 1.0 convolution_add_fusion.5
  354.4 1.0 convolution_add_fusion.4
  356.0 1.0 convolution_add_fusion.3
  362.4 52.1 %all-gather.17.cloned.1.call-done = bf16[8,1024,128]{2,0,1:T(8,128)(2,1)} async-done(((bf16[8,32,128]{2,0,1:T(8,128)(2,1)}), bf16[8,1024,128]{2,0,1:T(8,128)(2,1)}) %all-gather.17.cloned.1.call-update) | async-done | bytes 2097168 | tf_op jit(solution)/shard_map/all_gather | solution.py:98
  414.5 3.2 copy.55
  417.8 17.9 %all-gather.15.cloned.1.call-done = bf16[2,256,1024]{2,1,0:T(8,128)(2,1)} async-done(((bf16[2,256,256]{2,1,0:T(8,128)(2,1)}), bf16[2,256,1024]{2,1,0:T(8,128)(2,1)}) %all-gather.15.cloned.1.call-update) | async-done | bytes 1048592 | tf_op jit(solution)/shard_map/all_gather | solution.py:96
  435.7 2.5 fusion
  438.3 1.3 copy.57
  439.7 1.3 copy.56
  (83 shorter events, 17.9 us)
Async XLA Ops:
  7.2 52.1 %all-gather.7.cloned.1.call-start = ((), (), s32[]{:S(2)}) async-start(), calls=%async_computation.1 | async-start | bytes 2621440 | tf_op jit(solution)/shard_map/all_gather | solution.py:58
  7.9 127.3 %all-gather.9.cloned.1.call-start = ((), (), s32[]{:S(2)}) async-start(), calls=%async_computation.2 | async-start | bytes 2162688 | tf_op jit(solution)/shard_map/all_gather | solution.py:72
  9.5 184.3 %all-gather.11.cloned.1.call-start = ((), (), s32[]{:S(2)}) async-start(), calls=%async_computation.3 | async-start | bytes 3932160 | tf_op jit(solution)/shard_map/all_gather | solution.py:85
  59.2 4.5 %copy-start.1 = (bf16[1,1,2,8,2,32,2,512]{7,6,5,4,3,2,1,0:T(2,128)(2,1)S(1)}, bf16[1,1,2,8,2,32,2,512]{7,6,5,4,3,2,1,0:T(2,128)(2,1)}, u32[]{:S(2)}) copy-start(bf16[1,1,2,8,2,32,2,512]{7,6,5,4,3,2,1,0:T(2,128)(2,1)} %stack.142) | copy-start | bytes 6291460
  139.4 10.0 %copy-start.24 = (f32[27,32,256]{2,1,0:T(8,128)S(1)}, f32[27,32,256]{2,1,0:T(8,128)}, u32[]{:S(2)}) copy-start(f32[27,32,256]{2,1,0:T(8,128)} %param.8) | copy-start | bytes 2654212
  139.4 10.9 %copy-start.25 = (f32[8,32,128]{2,1,0:T(8,128)S(1)}, f32[8,32,128]{2,1,0:T(8,128)}, u32[]{:S(2)}) copy-start(f32[8,32,128]{2,1,0:T(8,128)} %param.9) | copy-start | bytes 393220
  139.5 7.9 %collective-permute-start.1 = (bf16[2,1,8,32,256]{4,3,2,0,1:T(8,128)(2,1)S(1)}, bf16[2,1,8,32,256]{4,3,2,0,1:T(8,128)(2,1)S(1)}, u32[]{:S(2)}, u32[]{:S(2)}) collective-permute-start(bf16[2,1,8,32,256]{4,3,2,0,1:T(8,128)(2,1)S(1)} %pad_maximum_fusion.10), channel_id=1, source_target_pairs={{1,0},{2,1},{3,2},{4,3},{5,4},{6,5},{7,6},{8,7},{9,8},{10,9},{11,1... | collective-permute-start | bytes 786440 | tf_op jit(solution)/shard_map/ppermute | solution.py:15
  141.0 7.3 %collective-permute-start = (bf16[2,1,8,32,256]{4,3,2,0,1:T(8,128)(2,1)S(1)}, bf16[2,1,8,32,256]{4,3,2,0,1:T(8,128)(2,1)S(1)}, u32[]{:S(2)}, u32[]{:S(2)}) collective-permute-start(bf16[2,1,8,32,256]{4,3,2,0,1:T(8,128)(2,1)S(1)} %pad_maximum_fusion.10), channel_id=1, source_target_pairs={{0,1},{1,2},{2,3},{3,4},{4,5},{5,6},{6,7},{7,8},{8,9},{9,10},{10,1... | collective-permute-start | bytes 786440 | tf_op jit(solution)/shard_map/ppermute | solution.py:12
  149.3 192.7 %all-gather.13.cloned.1.call-start = ((), (), s32[]{:S(2)}) async-start(), calls=%async_computation.4 | async-start | bytes 14598144 | tf_op jit(solution)/shard_map/all_gather | solution.py:88
  150.2 264.3 %all-gather.17.cloned.1.call-start = ((), (), s32[]{:S(2)}) async-start(), calls=%async_computation.6 | async-start | bytes 2162688 | tf_op jit(solution)/shard_map/all_gather | solution.py:98
  151.0 284.7 %all-gather.15.cloned.1.call-start = ((), (), s32[]{:S(2)}) async-start(), calls=%async_computation.5 | async-start | bytes 1310720 | tf_op jit(solution)/shard_map/all_gather | solution.py:96
  202.7 3.4 copy-start
  224.8 3.5 copy-start.11
  224.8 3.5 copy-start.12
  224.8 3.4 copy-start.13
  224.8 3.4 copy-start.14
  238.2 3.6 copy-start.6
  238.2 3.6 copy-start.7
  238.2 3.6 copy-start.8
  238.2 3.6 copy-start.9
  238.2 3.6 copy-start.10
  251.8 3.5 copy-start.2
  251.9 3.5 copy-start.3
  251.9 3.5 copy-start.4
  251.9 3.5 copy-start.5
  268.5 79.6 %copy-start.18 = (bf16[64,8,3,1024]{3,1,2,0:T(8,128)(2,1)S(1)}, bf16[64,8,3,1024]{3,1,2,0:T(8,128)(2,1)}, u32[]{:S(2)}) copy-start(bf16[64,8,3,1024]{3,1,2,0:T(8,128)(2,1)} %copy.60) | copy-start | bytes 9437188
  348.2 1.9 copy-start.19
  349.2 2.1 copy-start.22
  351.1 1.9 copy-start.23
  352.3 2.1 copy-start.20
  354.0 2.0 copy-start.21
  355.4 2.0 copy-start.17
  357.0 2.0 copy-start.15
  358.5 2.0 copy-start.16
Sparse Core Ops, SparseCore 0:
  9.7 48.0 all-gather.6
  61.1 74.1 all-gather.8
  149.4 44.3 all-gather.10
  197.2 144.7 all-gather.12
  345.5 69.0 all-gather.16
  416.6 19.0 all-gather.14
